TPU v7x, 128 devices: a whole 4x4x4 slice. The times are simulated.
128 devices in a mesh: dp: 8 (over z, core), table: 16 (over x, y).
Axes of the slice: x: 4, y: 4, z: 4, core: 2. Of those that a mesh axis runs over, the one named last changes fastest.
Arguments:
- values: bfloat16 [16384, 1024], P('table'), may hold values from -6 to 6
- first_moment: float32 [16384, 1024], P('table'), may hold values from -2 to 2
- second_moment: float32 [16384, 1024], P('table'), may hold values from 0.01 to 1
- grads: bfloat16 [1024, 64, 1024], P(('dp', 'table')), may hold values from -6 to 6
- block_ids: int32 [128, 8], P(('dp', 'table')), may hold values from 0 to 255, as said below
- live_counts: int32 [128], P(('dp', 'table')), may hold values from 4 to 8
- step_count: int32 [1], replicated, may hold values from 1 to 19
Outputs:
- new_values: bfloat16 [16384, 1024], P('table')
- new_first: float32 [16384, 1024], P('table')
- new_second: float32 [16384, 1024], P('table')
Inputs may be any that keep to these rules, and one draw needn't show every extreme that they name: `block_ids`: device h belongs to replica h // 16. Live ids of a device are ascending and lie in blocks of different owners (owner = id // 16), so one device sends at most one live block to any owner; in every draw some owner receives a live block from every device of a replica. The live ids of one replica name at most 2 different blocks of any one owner, and exactly 2 of some owner in every replica. Ids of dead slots are arbitrary blocks.
All inputs are finite; a program needn't handle non-finite values.
Results may differ from a plain program's by a relative error of at most 0.0004.
Values may be sent and summed in bfloat16 or wider, within the bound.
A program may use at most 128 MiB of HBM per device.

v0:
```python
import jax
import jax.numpy as jnp
from jax import lax
from jax.sharding import PartitionSpec as P

BROWS = 64
SLOTS = 8
KBLK = 2


def adam_rows(values, first_moment, second_moment, row_grad, row_hits, step_count):
    touched = (row_hits > 0.0)[:, None]
    beta_one = 0.9
    beta_two = 0.99
    steps_done = step_count[0].astype(jnp.float32)
    first_next = beta_one * first_moment + (1.0 - beta_one) * row_grad
    second_next = beta_two * second_moment + (1.0 - beta_two) * row_grad * row_grad
    first_hat = first_next / (1.0 - jnp.power(jnp.float32(beta_one), steps_done))
    second_hat = second_next / (1.0 - jnp.power(jnp.float32(beta_two), steps_done))
    moved = values.astype(jnp.float32) - 0.05 * first_hat / (jnp.sqrt(second_hat) + 1e-08)
    new_values = jnp.where(touched, moved.astype(jnp.bfloat16), values)
    new_first = jnp.where(touched, first_next, first_moment)
    new_second = jnp.where(touched, second_next, second_moment)
    return (new_values, new_first, new_second)


def per_device(values, first_moment, second_moment, grads, block_ids, live_counts, step_count):
    owners = lax.axis_size("table")
    own_rows = values.shape[0]
    width = values.shape[1]
    blk_here = own_rows // BROWS
    slot_ids = block_ids[0]
    live = jnp.arange(SLOTS, dtype=jnp.int32) < live_counts[0]
    owner_of = slot_ids // blk_here
    local_block = slot_ids % blk_here
    select = (owner_of[None, :] == jnp.arange(owners, dtype=jnp.int32)[:, None]) & live[None, :]
    outgoing = jnp.einsum(
        "os,sxd->oxd", select.astype(jnp.bfloat16), grads, preferred_element_type=jnp.float32
    ).astype(jnp.bfloat16)
    select_int = select.astype(jnp.int32)
    labels = jnp.stack(
        [jnp.sum(select_int * local_block[None, :], axis=1), jnp.sum(select_int, axis=1)], axis=1
    )
    incoming, arrived = (
        lax.all_to_all(outgoing, "table", split_axis=0, concat_axis=0, tiled=True),
        lax.all_to_all(labels, "table", split_axis=0, concat_axis=0, tiled=True),
    )
    matches = (arrived[:, 0][None, :] == jnp.arange(blk_here, dtype=jnp.int32)[:, None]) & (
        arrived[:, 1][None, :] == 1
    )
    block_hits = jnp.sum(matches.astype(jnp.float32), axis=1)
    touched_block = block_hits > 0.0
    order = jnp.cumsum(touched_block.astype(jnp.int32)) - 1
    packing = (
        (order[None, :] == jnp.arange(KBLK, dtype=jnp.int32)[:, None]) & touched_block[None, :]
    ).astype(jnp.float32)
    chooser = jnp.dot(packing, matches.astype(jnp.float32), precision=lax.Precision.HIGHEST).astype(
        jnp.bfloat16
    )
    packed = jnp.einsum("ks,sxd->kxd", chooser, incoming, preferred_element_type=jnp.float32)
    block_index = jnp.arange(blk_here, dtype=jnp.float32)
    packed_ids = jnp.sum(packing * (block_index[None, :] + 1.0), axis=1) - 1.0
    packed_hits = jnp.sum(packing * block_hits[None, :], axis=1)
    all_packed, all_ids, all_hits = (
        lax.all_gather(packed, "dp", axis=0, tiled=True),
        lax.all_gather(packed_ids, "dp", axis=0, tiled=True),
        lax.all_gather(packed_hits, "dp", axis=0, tiled=True),
    )
    placing = (all_ids[None, :] == block_index[:, None]).astype(jnp.float32)
    row_grad = jnp.einsum(
        "bk,kxd->bxd", placing, all_packed, precision=lax.Precision.HIGHEST
    ).reshape(own_rows, width)
    total_hits = jnp.repeat(jnp.sum(placing * all_hits[None, :], axis=1), BROWS)
    return adam_rows(values, first_moment, second_moment, row_grad, total_hits, step_count)


def solution(mesh):
    in_specs = (
        P("table", None),
        P("table", None),
        P("table", None),
        P(("dp", "table"), None, None),
        P(("dp", "table"), None),
        P(("dp", "table")),
        P(),
    )
    out_specs = (P("table", None), P("table", None), P("table", None))
    return jax.shard_map(
        per_device, mesh=mesh, in_specs=in_specs, out_specs=out_specs, check_vma=False
    )
```

profile of v0, /device:TPU:1, one launch (start us, length us, event | category | flops | bytes accessed | tf_op | source)
XLA Modules:
  0.0 118.3 jit_solution(3008917598142463513)
XLA Ops:
  7.9 0.7 fusion.24
  8.6 0.1 select_reduce_fusion.1
  8.7 0.7 copy.29
  9.4 7.6 %all-to-all-start = ((s32[16,1,2]{2,1,0:T(1,128)}), s32[16,1,2]{2,1,0:T(1,128)S(1)}, u32[]{:S(2)}, u32[]{:S(2)}) async-start(s32[16,1,2]{2,1,0:T(1,128)} %copy.29), calls=%async_computation | async-start | bytes 16384 | tf_op jit(solution)/shard_map/all_to_all | solution.py:46
  17.0 0.9 convolution_convert_fusion
  17.9 2.5 %copy.33 = bf16[16,64,1024]{2,1,0:T(8,128)(2,1)} copy(bf16[16,64,1024]{2,0,1:T(8,128)(2,1)S(1)} %convolution_convert_fusion) | data formatting | bytes 4194304 | tf_op jit(solution)/shard_map/convert_element_type | solution.py:39
  20.4 2.9 %all-to-all-done = s32[16,1,2]{2,1,0:T(1,128)S(1)} async-done(((s32[16,1,2]{2,1,0:T(1,128)}), s32[16,1,2]{2,1,0:T(1,128)S(1)}, u32[]{:S(2)}, u32[]{:S(2)}) %all-to-all-start) | async-done | bytes 160 | tf_op jit(solution)/shard_map/all_to_all | solution.py:46
  23.3 3.9 %all-to-all-start.1 = ((bf16[16,64,1024]{2,1,0:T(8,128)(2,1)}), bf16[16,64,1024]{2,1,0:T(8,128)(2,1)S(1)}, u32[]{:S(2)}, u32[]{:S(2)}) async-start(bf16[16,64,1024]{2,1,0:T(8,128)(2,1)} %copy.33), calls=%async_computation.1 | async-start | bytes 4194304 | tf_op jit(solution)/shard_map/all_to_all | solution.py:45
  27.2 0.0 all-gather.2.cloned.1.call-start
  27.2 0.1 copy.30
  27.3 0.1 convert_reduce_fusion
  27.4 0.1 copy.31
  27.6 0.1 add_reduce_fusion
  27.7 0.1 fusion.9
  27.8 24.9 %all-to-all-done.1 = bf16[16,64,1024]{2,1,0:T(8,128)(2,1)S(1)} async-done(((bf16[16,64,1024]{2,1,0:T(8,128)(2,1)}), bf16[16,64,1024]{2,1,0:T(8,128)(2,1)S(1)}, u32[]{:S(2)}, u32[]{:S(2)}) %all-to-all-start.1) | async-done | bytes 2097184 | tf_op jit(solution)/shard_map/all_to_all | solution.py:45
  52.7 1.3 %fusion.7 = f32[2,64,1024]{2,0,1:T(2,128)S(1)} fusion(bf16[2,16,1]{1,0,2:T(2,128)(2,1)S(1)} %fusion.9, bf16[16,64,1024]{2,1,0:T(8,128)(2,1)S(1)} %all-to-all-done.1), kind=kOutput, calls=%fused_computation.10 | convolution fusion | flops 4194304 | bytes 2621504 | tf_op jit(solution)/shard_map/ks,sxd->kxd/dot_general | solution.py:60
  54.0 1.0 copy.35
  55.0 0.0 all-gather.2.cloned.1.call-update
  55.7 0.6 dynamic-slice
  57.0 0.1 select_reduce_fusion.2
  57.1 0.2 dynamic-update-slice.1
  57.4 0.1 add_dynamic-update-slice_fusion
  57.5 18.8 %all-reduce.2 = (f32[16]{0:T(128)S(1)}, f32[16]{0:T(128)S(1)}) all-reduce(f32[16]{0:T(128)S(1)} %add_dynamic-update-slice_fusion, f32[16]{0:T(128)S(1)} %dynamic-update-slice.1), channel_id=1, replica_groups=mesh['dp'=8,'table'=16] {'dp'}, use_global_device_ids=true, to_apply=%add | all-reduce | flops 32 | bytes 256
  76.2 0.1 select_reduce_fusion
  76.4 0.1 broadcast_in_dim.13
  76.4 0.1 gt.31
  76.5 15.0 %all-gather.2.cloned.1.call-done = f32[16,64,1024]{2,1,0:T(8,128)} async-done(((f32[2,64,1024]{2,1,0:T(8,128)}), f32[16,64,1024]{2,1,0:T(8,128)}) %all-gather.2.cloned.1.call-update) | async-done | bytes 4194320 | tf_op jit(solution)/shard_map/all_gather | solution.py:65
  91.5 6.6 %fusion.2 = f32[16,64,1024]{2,0,1:T(8,128)S(1)} fusion(f32[16,64,1024]{2,1,0:T(8,128)} %all-gather.2.cloned.1.call-done, f32[16]{0:T(128)S(1)} %get-tuple-element.7), kind=kOutput, calls=%fused_computation.4 | convolution fusion | flops 201326848 | bytes 8388672 | tf_op jit(solution)/shard_map/bk,kxd->bxd/dot_general | solution.py:70
  98.1 2.4 %copy.37 = f32[16,64,1024]{2,1,0:T(8,128)S(1)} copy(f32[16,64,1024]{2,0,1:T(8,128)S(1)} %fusion.2) | data formatting | bytes 8388608 | tf_op jit(solution)/shard_map/bk,kxd->bxd/dot_general | solution.py:70
  100.5 1.0 copy-done.2
  101.5 4.7 %fusion.5 = (f32[1024,1024]{1,0:T(8,128)}, f32[1024,1024]{1,0:T(8,128)}) fusion(f32[1024,1024]{1,0:T(8,128)S(1)} %copy-done.1, f32[16,64,1024]{2,1,0:T(8,128)S(1)} %copy.37, pred[1024]{0:T(1024)(128)(4,1)S(1)} %gt.31, f32[1024,1024]{1,0:T(8,128)S(1)} %copy-done.2), kind=kLoop, calls=%fused_computation.8 | loop fusion | flops 9437184 | bytes 20972544 | tf_op jit(solution)/shard_map/jit(_where)/select_n | solution.py:23
  106.3 5.2 %fusion.6 = bf16[1024,1024]{1,0:T(8,128)(2,1)} fusion(bf16[1024,1024]{1,0:T(8,128)(2,1)S(1)} %copy-done.3, f32[1024,1024]{1,0:T(8,128)S(1)} %copy-done.1, f32[16,64,1024]{2,1,0:T(8,128)S(1)} %copy.37, f32[1024,1024]{1,0:T(8,128)S(1)} %copy-done.2, f32[]{:T(128)} %bitcast.16, f32[]{:T(128)} %bitcast.15, pred[1024]{0:T(1024)(128)(4,1)S(1)} %gt.31), kind=kLoop, calls=%fused_computation.9 | loop fusion | flops 16777216 | bytes 16778248 | tf_op jit(solution)/shard_map/jit(_where)/select_n | solution.py:21
  (19 shorter events, 0.1 us)
Async XLA Ops:
  7.2 9.8 %copy-start = (bf16[8,64,1024]{2,1,0:T(8,128)(2,1)S(1)}, bf16[8,64,1024]{2,1,0:T(8,128)(2,1)}, u32[]{:S(2)}) copy-start(bf16[8,64,1024]{2,1,0:T(8,128)(2,1)} %param.10) | copy-start | bytes 3145732
  9.4 13.9 %all-to-all-start = ((s32[16,1,2]{2,1,0:T(1,128)}), s32[16,1,2]{2,1,0:T(1,128)S(1)}, u32[]{:S(2)}, u32[]{:S(2)}) async-start(s32[16,1,2]{2,1,0:T(1,128)} %copy.29), calls=%async_computation | async-start | bytes 16384 | tf_op jit(solution)/shard_map/all_to_all | solution.py:46
  20.4 35.3 %copy-start.4 = (u32[128]{0:T(128)S(1)}, u32[128]{0:T(128)}, u32[]{:S(2)}) copy-start(u32[128]{0:T(128)} %constant.75) | copy-start | bytes 1540
  23.3 29.4 %all-to-all-start.1 = ((bf16[16,64,1024]{2,1,0:T(8,128)(2,1)}), bf16[16,64,1024]{2,1,0:T(8,128)(2,1)S(1)}, u32[]{:S(2)}, u32[]{:S(2)}) async-start(bf16[16,64,1024]{2,1,0:T(8,128)(2,1)} %copy.33), calls=%async_computation.1 | async-start | bytes 4194304 | tf_op jit(solution)/shard_map/all_to_all | solution.py:45
  27.2 64.3 %all-gather.2.cloned.1.call-start = ((), (), s32[]{:S(2)}) async-start(), calls=%async_computation.2 | async-start | bytes 4718592 | tf_op jit(solution)/shard_map/all_gather | solution.py:65
  98.1 2.5 %copy-start.1 = (f32[1024,1024]{1,0:T(8,128)S(1)}, f32[1024,1024]{1,0:T(8,128)}, u32[]{:S(2)}) copy-start(f32[1024,1024]{1,0:T(8,128)} %param.9) | copy-start | bytes 12582916
  98.1 3.5 %copy-start.2 = (f32[1024,1024]{1,0:T(8,128)S(1)}, f32[1024,1024]{1,0:T(8,128)}, u32[]{:S(2)}) copy-start(f32[1024,1024]{1,0:T(8,128)} %param.8) | copy-start | bytes 12582916
  101.5 4.7 %copy-start.3 = (bf16[1024,1024]{1,0:T(8,128)(2,1)S(1)}, bf16[1024,1024]{1,0:T(8,128)(2,1)}, u32[]{:S(2)}) copy-start(bf16[1024,1024]{1,0:T(8,128)(2,1)} %param.7) | copy-start | bytes 6291460
Sparse Core Ops, SparseCore 0:
  55.1 36.3 all-gather.1
where the time goes:
time: 119 us; the launch traced here: 118 us
  waiting for transfers between devices  42.8 us (36%)
  blocking collectives  18.8 us (16%)
  between operations  16.3 us (14%)
  starting transfers between devices  11.5 us (10%)
  other arithmetic  11.4 us (10%)
  matrix products  8.89 us (7%)
  local copies, waits for them, and re-layouts  8.73 us (7%)
    all_to_all x1, waiting for transfers between devices, per_device(): lax.all_to_all(outgoing, 'table', split_axis=0, concat_axis=0, tiled=True)  24.9 us
    unnamed x1, blocking collectives  18.8 us
    all_gather x1, waiting for transfers between devices, per_device(): lax.all_gather(packed, 'dp', axis=0, tiled=True)  15 us
    all_to_all x1, starting transfers between devices, per_device(): lax.all_to_all(labels, 'table', split_axis=0, concat_axis=0, tiled=True)  7.58 us
    dot_general x1, matrix products, per_device(): jnp.einsum('bk,kxd->bxd', placing, all_packed, precision=lax.Precision.HI...  6.56 us
    select_n x1, other arithmetic, adam_rows(): new_values = jnp.where(touched, moved.astype(jnp.bfloat16), values)  5.21 us
    select_n x1, other arithmetic, adam_rows(): new_second = jnp.where(touched, second_next, second_moment)  4.72 us
    all_to_all x1, starting transfers between devices, per_device(): lax.all_to_all(outgoing, 'table', split_axis=0, concat_axis=0, tiled=True)  3.86 us
  transfers between devices with their start and end apart: 3, of which 3 were waited for; matrix products, arithmetic and copies ran while one was open for 5% of the time, Pallas kernels for 0%

commit v1 on v0

--- a/solution.py
+++ b/solution.py
@@ -62,7 +62,9 @@
     packed_ids = jnp.sum(packing * (block_index[None, :] + 1.0), axis=1) - 1.0
     packed_hits = jnp.sum(packing * block_hits[None, :], axis=1)
     all_packed, all_ids, all_hits = (
-        lax.all_gather(packed, "dp", axis=0, tiled=True),
+        jnp.concatenate(
+            lax.all_to_all(jnp.stack([packed] * lax.axis_size("dp")), "dp", 0, 0), axis=0
+        ),
         lax.all_gather(packed_ids, "dp", axis=0, tiled=True),
         lax.all_gather(packed_hits, "dp", axis=0, tiled=True),
     )

time: 119 us -> 146 us (1.23)
  blocking collectives: 18.8 us -> 50.6 us
  local copies, waits for them, and re-layouts: 8.73 us -> 24.1 us
  waiting for transfers between devices: 42.8 us -> 27.9 us
  between operations: 16.3 us -> 2.87 us
  starting transfers between devices: 11.5 us -> 21.9 us
  matrix products: 8.89 us -> 6.59 us
    unnamed x1, blocking collectives: 18.8 us -> 50.6 us
    all_gather x1 -> x0, waiting for transfers between devices: 15 us -> none  [per_device(): lax.all_gather(packed, 'dp', axis=0, tiled=True)]
    all_to_all x0 -> x1, starting transfers between devices: none -> 10.6 us  [per_device(): lax.all_to_all(jnp.stack([packed] * lax.axis_size('dp')), 'dp', 0, 0)]
    all_to_all x0 -> x1, local copies, waits for them, and re-layouts: none -> 6.82 us  [per_device(): lax.all_to_all(jnp.stack([packed] * lax.axis_size('dp')), 'dp', 0, 0)]
    reshape x0 -> x1, local copies, waits for them, and re-layouts: none -> 6.04 us  [per_device(): jnp.concatenate(lax.all_to_all(jnp.stack([packed] * lax.axis_size('dp')),...]
    another operation x0 -> x1, local copies, waits for them, and re-layouts: none -> 3.45 us  [per_device(): jnp.stack([packed] * lax.axis_size('dp'))]
    dot_general x1, matrix products: 6.56 us -> 4.26 us  [per_device(): jnp.einsum('bk,kxd->bxd', placing, all_packed, precision=lax.Precision.HI...]
  transfers between devices with their start and end apart: 3 -> 3, of which waited for: 3 -> 2; matrix products, arithmetic and copies ran while one was open for 5% -> 4% of each run, Pallas kernels for 0% -> 0%
where the time goes in v1:
time: 146 us; the launch traced here: 145 us
  blocking collectives  50.6 us (35%)
  waiting for transfers between devices  27.9 us (19%)
  local copies, waits for them, and re-layouts  24.1 us (17%)
  starting transfers between devices  21.9 us (15%)
  other arithmetic  11.4 us (8%)
  matrix products  6.59 us (5%)
  between operations  2.87 us (2%)
    unnamed x1, blocking collectives  50.6 us
    all_to_all x1, waiting for transfers between devices, per_device(): lax.all_to_all(outgoing, 'table', split_axis=0, concat_axis=0, tiled=True)  25 us
    all_to_all x1, starting transfers between devices, per_device(): lax.all_to_all(jnp.stack([packed] * lax.axis_size('dp')), 'dp', 0, 0)  10.6 us
    all_to_all x1, starting transfers between devices, per_device(): lax.all_to_all(labels, 'table', split_axis=0, concat_axis=0, tiled=True)  7.58 us
    all_to_all x1, local copies, waits for them, and re-layouts, per_device(): lax.all_to_all(jnp.stack([packed] * lax.axis_size('dp')), 'dp', 0, 0)  6.82 us
    reshape x1, local copies, waits for them, and re-layouts, per_device(): jnp.concatenate(lax.all_to_all(jnp.stack([packed] * lax.axis_size('dp')),...  6.04 us
    select_n x1, other arithmetic, adam_rows(): new_values = jnp.where(touched, moved.astype(jnp.bfloat16), values)  5.21 us
    select_n x1, other arithmetic, adam_rows(): new_second = jnp.where(touched, second_next, second_moment)  4.72 us
  transfers between devices with their start and end apart: 3, of which 2 were waited for; matrix products, arithmetic and copies ran while one was open for 4% of the time, Pallas kernels for 0%

profile of v1, /device:TPU:1, one launch (start us, length us, event | category | flops | bytes accessed | tf_op | source)
XLA Modules:
  0.0 145.3 jit_solution(3138446018042766129)
XLA Ops:
  1.4 0.7 fusion.23
  2.1 0.1 select_reduce_fusion.1
  2.2 0.7 copy.21
  2.8 7.6 %all-to-all-start = ((s32[16,1,2]{2,1,0:T(1,128)}), s32[16,1,2]{2,1,0:T(1,128)S(1)}, u32[]{:S(2)}, u32[]{:S(2)}) async-start(s32[16,1,2]{2,1,0:T(1,128)} %copy.21), calls=%async_computation | async-start | bytes 16384 | tf_op jit(solution)/shard_map/all_to_all | solution.py:46
  10.4 0.9 convolution_convert_fusion
  11.4 2.5 %copy.25 = bf16[16,64,1024]{2,1,0:T(8,128)(2,1)} copy(bf16[16,64,1024]{2,0,1:T(8,128)(2,1)S(1)} %convolution_convert_fusion) | data formatting | bytes 4194304 | tf_op jit(solution)/shard_map/convert_element_type | solution.py:39
  13.8 2.9 %all-to-all-done = s32[16,1,2]{2,1,0:T(1,128)S(1)} async-done(((s32[16,1,2]{2,1,0:T(1,128)}), s32[16,1,2]{2,1,0:T(1,128)S(1)}, u32[]{:S(2)}, u32[]{:S(2)}) %all-to-all-start) | async-done | bytes 160 | tf_op jit(solution)/shard_map/all_to_all | solution.py:46
  16.8 3.7 %all-to-all-start.1 = ((bf16[16,64,1024]{2,1,0:T(8,128)(2,1)}), bf16[16,64,1024]{2,1,0:T(8,128)(2,1)S(1)}, u32[]{:S(2)}, u32[]{:S(2)}) async-start(bf16[16,64,1024]{2,1,0:T(8,128)(2,1)} %copy.25), calls=%async_computation.1 | async-start | bytes 4194304 | tf_op jit(solution)/shard_map/all_to_all | solution.py:45
  20.5 0.1 copy.22
  20.6 0.1 convert_reduce_fusion
  20.7 0.1 copy.23
  20.9 0.1 add_reduce_fusion
  21.0 0.1 fusion.7
  21.1 25.0 %all-to-all-done.1 = bf16[16,64,1024]{2,1,0:T(8,128)(2,1)S(1)} async-done(((bf16[16,64,1024]{2,1,0:T(8,128)(2,1)}), bf16[16,64,1024]{2,1,0:T(8,128)(2,1)S(1)}, u32[]{:S(2)}, u32[]{:S(2)}) %all-to-all-start.1) | async-done | bytes 2097184 | tf_op jit(solution)/shard_map/all_to_all | solution.py:45
  46.1 1.3 fusion.5
  47.3 3.4 %stack.11 = f32[8,2,64,1024]{3,1,2,0:T(2,128)} broadcast(f32[2,64,1024]{2,0,1:T(2,128)S(1)} %fusion.5), dimensions={1,2,3} | broadcast | bytes 4718592 | tf_op jit(solution)/shard_map/stack | solution.py:66
  50.8 10.6 %all-to-all-start.2 = ((f32[8,2,64,1024]{3,1,2,0:T(2,128)}), f32[8,2,64,1024]{3,1,2,0:T(2,128)}, u32[]{:S(2)}, u32[]{:S(2)}) async-start(f32[8,2,64,1024]{3,1,2,0:T(2,128)} %stack.11), calls=%async_computation.2 | async-start | bytes 8388608 | tf_op jit(solution)/shard_map/all_to_all | solution.py:66
  62.1 0.6 dynamic-slice
  63.4 0.1 select_reduce_fusion.2
  63.5 0.2 dynamic-update-slice.1
  63.8 0.1 add_dynamic-update-slice_fusion
  63.9 50.6 %all-reduce.2 = (f32[16]{0:T(128)S(1)}, f32[16]{0:T(128)S(1)}) all-reduce(f32[16]{0:T(128)S(1)} %add_dynamic-update-slice_fusion, f32[16]{0:T(128)S(1)} %dynamic-update-slice.1), channel_id=1, replica_groups=mesh['dp'=8,'table'=16] {'dp'}, use_global_device_ids=true, to_apply=%add | all-reduce | flops 32 | bytes 256
  114.4 0.1 select_reduce_fusion
  114.6 0.1 broadcast_in_dim.13
  114.7 0.1 gt.31
  114.7 6.8 %copy.27 = f32[8,2,64,1024]{3,1,0,2:T(2,128)} copy(f32[8,2,64,1024]{3,1,2,0:T(2,128)} %all-to-all-done.2) | data formatting | bytes 8388608 | tf_op jit(solution)/shard_map/all_to_all | solution.py:66
  121.6 6.0 %reshape.95 = f32[16,64,1024]{2,0,1:T(8,128)} reshape(f32[8,2,64,1024]{3,1,0,2:T(2,128)} %copy.27) | data formatting | bytes 8388608 | tf_op jit(solution)/shard_map/reshape | solution.py:65
  127.6 4.3 %fusion.12 = f32[16,64,1024]{2,0,1:T(8,128)S(1)} fusion(f32[16,64,1024]{2,0,1:T(8,128)} %reshape.95, f32[16]{0:T(128)S(1)} %get-tuple-element.7), kind=kOutput, calls=%fused_computation.21 | convolution fusion | flops 201326848 | bytes 8388672 | tf_op jit(solution)/shard_map/bk,kxd->bxd/dot_general | solution.py:72
  131.9 2.4 %copy.28 = f32[16,64,1024]{2,1,0:T(8,128)S(1)} copy(f32[16,64,1024]{2,0,1:T(8,128)S(1)} %fusion.12) | data formatting | bytes 8388608 | tf_op jit(solution)/shard_map/bk,kxd->bxd/dot_general | solution.py:72
  134.3 1.0 copy-done.2
  135.3 4.7 %fusion.3 = (f32[1024,1024]{1,0:T(8,128)}, f32[1024,1024]{1,0:T(8,128)}) fusion(f32[1024,1024]{1,0:T(8,128)S(1)} %copy-done.1, f32[16,64,1024]{2,1,0:T(8,128)S(1)} %copy.28, pred[1024]{0:T(1024)(128)(4,1)S(1)} %gt.31, f32[1024,1024]{1,0:T(8,128)S(1)} %copy-done.2), kind=kLoop, calls=%fused_computation.6 | loop fusion | flops 9437184 | bytes 20972544 | tf_op jit(solution)/shard_map/jit(_where)/select_n | solution.py:23
  140.1 5.2 %fusion.4 = bf16[1024,1024]{1,0:T(8,128)(2,1)} fusion(bf16[1024,1024]{1,0:T(8,128)(2,1)S(1)} %copy-done.3, f32[1024,1024]{1,0:T(8,128)S(1)} %copy-done.1, f32[16,64,1024]{2,1,0:T(8,128)S(1)} %copy.28, f32[1024,1024]{1,0:T(8,128)S(1)} %copy-done.2, f32[]{:T(128)} %bitcast.16, f32[]{:T(128)} %bitcast.15, pred[1024]{0:T(1024)(128)(4,1)S(1)} %gt.31), kind=kLoop, calls=%fused_computation.7 | loop fusion | flops 16777216 | bytes 16778248 | tf_op jit(solution)/shard_map/jit(_where)/select_n | solution.py:21
  (20 shorter events, 0.1 us)
Async XLA Ops:
  0.6 9.8 %copy-start = (bf16[8,64,1024]{2,1,0:T(8,128)(2,1)S(1)}, bf16[8,64,1024]{2,1,0:T(8,128)(2,1)}, u32[]{:S(2)}) copy-start(bf16[8,64,1024]{2,1,0:T(8,128)(2,1)} %param.10) | copy-start | bytes 3145732
  2.8 13.9 %all-to-all-start = ((s32[16,1,2]{2,1,0:T(1,128)}), s32[16,1,2]{2,1,0:T(1,128)S(1)}, u32[]{:S(2)}, u32[]{:S(2)}) async-start(s32[16,1,2]{2,1,0:T(1,128)} %copy.21), calls=%async_computation | async-start | bytes 16384 | tf_op jit(solution)/shard_map/all_to_all | solution.py:46
  16.8 29.3 %all-to-all-start.1 = ((bf16[16,64,1024]{2,1,0:T(8,128)(2,1)}), bf16[16,64,1024]{2,1,0:T(8,128)(2,1)S(1)}, u32[]{:S(2)}, u32[]{:S(2)}) async-start(bf16[16,64,1024]{2,1,0:T(8,128)(2,1)} %copy.25), calls=%async_computation.1 | async-start | bytes 4194304 | tf_op jit(solution)/shard_map/all_to_all | solution.py:45
  50.8 11.3 %copy-start.4 = (u32[128]{0:T(128)S(1)}, u32[128]{0:T(128)}, u32[]{:S(2)}) copy-start(u32[128]{0:T(128)} %constant.75) | copy-start | bytes 1540
  50.8 63.9 %all-to-all-start.2 = ((f32[8,2,64,1024]{3,1,2,0:T(2,128)}), f32[8,2,64,1024]{3,1,2,0:T(2,128)}, u32[]{:S(2)}, u32[]{:S(2)}) async-start(f32[8,2,64,1024]{3,1,2,0:T(2,128)} %stack.11), calls=%async_computation.2 | async-start | bytes 8388608 | tf_op jit(solution)/shard_map/all_to_all | solution.py:66
  131.9 2.5 %copy-start.1 = (f32[1024,1024]{1,0:T(8,128)S(1)}, f32[1024,1024]{1,0:T(8,128)}, u32[]{:S(2)}) copy-start(f32[1024,1024]{1,0:T(8,128)} %param.9) | copy-start | bytes 12582916
  131.9 3.5 %copy-start.2 = (f32[1024,1024]{1,0:T(8,128)S(1)}, f32[1024,1024]{1,0:T(8,128)}, u32[]{:S(2)}) copy-start(f32[1024,1024]{1,0:T(8,128)} %param.8) | copy-start | bytes 12582916
  135.3 4.7 %copy-start.3 = (bf16[1024,1024]{1,0:T(8,128)(2,1)S(1)}, bf16[1024,1024]{1,0:T(8,128)(2,1)}, u32[]{:S(2)}) copy-start(bf16[1024,1024]{1,0:T(8,128)(2,1)} %param.7) | copy-start | bytes 6291460
